TPU v7x, 256 devices: a whole 4x4x8 slice. The times are simulated.
256 devices in a mesh: train: 16 (over z, core), query: 16 (over y, x).
Axes of the slice: x: 4, y: 4, z: 8, core: 2. Of those that a mesh axis runs over, the one named last changes fastest.
Arguments:
- train_hidden: bfloat16 [512, 96, 4096], P(('train', 'query')), may hold values from -6 to 6
- train_outgrad: bfloat16 [512, 96, 14336], P(('train', 'query')), may hold values from -6 to 6
- train_mask: int32 [512, 96], P(('train', 'query')), may hold values 0 or 1
- query_hidden: bfloat16 [256, 96, 4096], P(('train', 'query')), may hold values from -6 to 6
- query_outgrad: bfloat16 [256, 96, 14336], P(('train', 'query')), may hold values from -6 to 6
- query_mask: int32 [256, 96], P(('train', 'query')), may hold values 0 or 1
- proj_in: bfloat16 [4096, 64], replicated, may hold values from -0.09375 to 0.09375
- proj_out: bfloat16 [14336, 64], replicated, may hold values from -0.046875 to 0.046875
Outputs:
- scores: float32 [512, 256], P(('train', 'query'))
All inputs are finite; a program needn't handle non-finite values. No bound on the sum of `train_mask` or of `query_mask` on one device may be relied on, other than what follows from the above.
Results may differ from a plain program's by a relative error of at most 0.0003.
Values sent between devices are 32-bit elements; how exact they have to be, the bound alone decides.
A program may use at most 128 MiB of HBM per device.

v0:
```python
import jax
import jax.numpy as jnp
from jax import lax
from jax.sharding import PartitionSpec as P

damping_share = 0.1
AXES = ("train", "query")
HIGHEST = lax.Precision.HIGHEST


def sketch_terms(hidden, outgrad, mask, proj_in, proj_out):
    proof_count, token_count, model_width = hidden.shape
    input_side = jnp.dot(
        hidden.reshape(proof_count * token_count, model_width),
        proj_in,
        preferred_element_type=jnp.float32,
    )
    output_side = jnp.dot(
        outgrad.reshape(proof_count * token_count, -1), proj_out, preferred_element_type=jnp.float32
    )
    output_side = output_side * mask.reshape(-1, 1).astype(jnp.float32)
    input_side = input_side.reshape(proof_count, token_count, -1)
    output_side = output_side.reshape(proof_count, token_count, -1)
    outer_sum = jnp.einsum("pti,ptj->pij", output_side, input_side, precision=HIGHEST)
    return outer_sum.reshape(proof_count, -1)


def spd_solve(system, right, tolerance=1e-3, most_steps=48):
    size = system.shape[0]
    eye = jnp.eye(size, dtype=system.dtype)
    diagonal = jnp.sum(system * eye, axis=1)
    inv_sqrt = lax.rsqrt(diagonal)
    bound = jnp.max(jnp.sum(jnp.abs(system) * inv_sqrt[:, None] * inv_sqrt[None, :], axis=1))
    start = eye * (1.0 / (diagonal * bound))[None, :]

    def going(carry):
        step, _, residual = carry
        return (step < most_steps) & (residual > tolerance)

    def one_step(inverse):
        remainder = eye - jnp.dot(system, inverse, precision=HIGHEST)
        residual = jnp.sqrt(jnp.sum(remainder * remainder))
        return inverse + jnp.dot(inverse, remainder, precision=HIGHEST), residual

    def advance(carry):
        step, inverse, _ = carry
        inverse, _ = one_step(inverse)
        inverse, residual = one_step(inverse)
        return step + 2, inverse, residual

    _, inverse, _ = lax.while_loop(
        going, advance, (jnp.int32(0), start, jnp.array(jnp.inf, system.dtype))
    )
    solved = jnp.dot(inverse, right, precision=HIGHEST)
    return solved + jnp.dot(
        inverse, right - jnp.dot(system, solved, precision=HIGHEST), precision=HIGHEST
    )


def body(
    train_hidden,
    train_outgrad,
    train_mask,
    query_hidden,
    query_outgrad,
    query_mask,
    proj_in,
    proj_out,
):
    train_sketch = sketch_terms(train_hidden, train_outgrad, train_mask, proj_in, proj_out)
    query_sketch = sketch_terms(query_hidden, query_outgrad, query_mask, proj_in, proj_out)
    block_rows = train_sketch.shape[0]
    width = train_sketch.shape[1]
    both = jnp.concatenate([train_sketch, query_sketch], axis=0)
    within = lax.all_gather(both.reshape(1, -1), AXES[1], axis=0, tiled=True)
    everyone = lax.all_gather(within, AXES[0], axis=0, tiled=True)
    devices = everyone.shape[0]
    pieces = [everyone[:, r * width:(r + 1) * width] for r in range(block_rows + 1)]
    all_train = jnp.concatenate(pieces[:block_rows], axis=0)
    gram_matrix = jnp.dot(all_train, all_train.T, precision=HIGHEST)
    products = jnp.dot(all_train, pieces[block_rows].T, precision=HIGHEST)
    total_rows = gram_matrix.shape[0]
    eye = jnp.eye(total_rows, dtype=jnp.float32)
    damping = damping_share * jnp.sum(gram_matrix * eye) / total_rows
    system = gram_matrix + damping * eye
    system, products = lax.optimization_barrier((system, products))
    solved = total_rows * spd_solve(system, products)
    me = lax.axis_index(AXES)
    return jnp.concatenate(
        [lax.dynamic_slice_in_dim(solved, r * devices + me, 1, 0) for r in range(block_rows)],
        axis=0,
    )


def solution(mesh):
    in_specs = (
        P(AXES, None, None),
        P(AXES, None, None),
        P(AXES, None),
        P(AXES, None, None),
        P(AXES, None, None),
        P(AXES, None),
        P(),
        P(),
    )
    out_specs = P(AXES, None)
    return jax.shard_map(body, mesh=mesh, in_specs=in_specs, out_specs=out_specs, check_vma=False)
```

profile of v0, /device:TPU:1, one launch (start us, length us, event | category | flops | bytes accessed | tf_op | source)
XLA Modules:
  0.0 260.9 jit_solution(17452568302198968251)
XLA Ops:
  6.5 0.0 copy-start
  6.5 0.0 all-gather.3.cloned.1.call-start
  6.5 0.8 convert_bitcast_fusion
  7.3 0.7 convert_element_type.28
  8.1 0.1 convert_element_type.29
  8.1 1.6 fusion.13
  9.8 0.0 copy-done
  9.8 2.4 fusion.9
  12.2 0.2 fusion.22
  12.4 0.1 reshape.66
  12.5 0.0 copy-start.7
  12.5 5.1 %convolution_multiply_fusion = f32[192,64]{0,1:T(8,128)S(1)} fusion(bf16[192,14336]{1,0:T(8,128)(2,1)} %bitcast.67, bf16[14336,64]{0,1:T(8,128)(2,1)} %param.17, f32[192]{0:T(256)S(1)} %convert_element_type.29), kind=kOutput, calls=%fused_computation.18 | convolution fusion | flops 352333824 | bytes 7389952 | tf_op jit(solution)/shard_map/dot_general | solution.py:18
  17.6 0.1 reshape.62
  17.7 2.1 fusion.15
  19.8 0.2 fusion.17
  20.0 0.1 reshape.63
  20.2 0.1 reshape.68
  20.2 20.5 %all-gather = f32[16,1,12288]{2,1,0:T(1,128)S(1)} all-gather(f32[1,1,12288]{2,1,0:T(1,128)S(1)} %reshape.68), channel_id=1, replica_groups=mesh['train'=16,'query'=16] {'query'}, dimensions={0}, use_global_device_ids=true | all-gather | bytes 835584 | tf_op jit(solution)/shard_map/all_gather | solution.py:75
  40.7 1.4 copy.20
  42.1 0.0 all-gather.3.cloned.1.call-update
  42.1 82.2 %all-gather.3.cloned.1.call-done = f32[256,12288]{1,0:T(8,128)} async-done(((f32[16,12288]{1,0:T(8,128)}), f32[256,12288]{1,0:T(8,128)}) %all-gather.3.cloned.1.call-update) | async-done | bytes 12582928 | tf_op jit(solution)/shard_map/all_gather | solution.py:76
  124.3 4.0 %fusion.21 = (f32[256,4096]{1,0:T(8,128)S(1)}, f32[256,4096]{1,0:T(8,128)S(1)}) fusion(f32[256,12288]{1,0:T(8,128)} %all-gather.3.cloned.1.call-done), kind=kLoop, calls=%fused_computation.41 | loop fusion | bytes 16777216 | tf_op jit(solution)/shard_map/slice | solution.py:78
  128.4 15.9 %select_reduce_fusion.1 = (f32[]{:T(128)}, f32[512,512]{1,0:T(8,128)}) fusion(f32[256,4096]{1,0:T(8,128)S(1)} %get-tuple-element.83, f32[256,4096]{1,0:T(8,128)S(1)} %get-tuple-element.82), kind=kOutput, calls=%fused_computation.23 | convolution fusion | flops 12887785472 | bytes 9437188 | tf_op jit(solution)/shard_map/dot_general | solution.py:80
  144.3 0.0 copy-done.5
  144.9 1.3 select_add_fusion
  146.3 0.0 copy-start.2
  146.3 10.6 %fusion.3 = f32[512,256]{1,0:T(8,128)S(1)} fusion(f32[256,4096]{1,0:T(8,128)} %copy-done.6, f32[256,4096]{1,0:T(8,128)} %copy-done.5, f32[256,12288]{1,0:T(8,128)} %all-gather.3.cloned.1.call-done), kind=kOutput, calls=%fused_computation.10 | convolution fusion | flops 6444548096 | bytes 13107200 | tf_op jit(solution)/shard_map/dot_general | solution.py:81
  156.9 0.1 select_reduce_fusion
  157.0 0.3 multiply_reduce_fusion.1
  157.3 0.6 reduce_max.9
  158.0 0.6 multiply_divide_fusion
  158.6 1.1 fusion.12
  159.7 2.5 copy.14
  162.3 84.0 %while.14 = (s32[]{:T(128)}, f32[512,512]{0,1:T(8,128)}, f32[]{:T(128)}, f32[512,512]{1,0:T(8,128)}, s32[]{:T(128)}) while((s32[]{:T(128)}, f32[512,512]{0,1:T(8,128)}, f32[]{:T(128)}, f32[512,512]{1,0:T(8,128)}, s32[]{:T(128)}) %tuple.39), condition=%wide.region_6.0_spmd.clone.clone, body=%wide.region_4.0_spmd.clone.clone.sunk | while | flops 6445072384 | bytes 20971660 | solution.py:51
  162.3 3.5 %convert_subtract_fusion.3 = f32[512,512]{0,1:T(8,128)S(1)} fusion(f32[512,512]{1,0:T(8,128)} %get-tuple-element.129, f32[512,512]{0,1:T(8,128)} %get-tuple-element.122), kind=kOutput, calls=%fused_computation.3.clone.1 | convolution fusion | flops 1611399168 | bytes 3145728 | tf_op jit(solution)/shard_map/while/body/dot_general | solution.py:41
  165.8 3.4 %fusion.63 = f32[512,512]{0,1:T(8,128)S(1)} fusion(f32[512,512]{0,1:T(8,128)} %get-tuple-element.122, f32[512,512]{0,1:T(8,128)S(1)} %convert_subtract_fusion.3), kind=kOutput, calls=%fused_computation.6.clone.1 | convolution fusion | flops 1610874880 | bytes 3145728 | tf_op jit(solution)/shard_map/while/body/dot_general | solution.py:43
  169.2 1.0 copy-done.1
  170.2 3.5 %multiply_reduce_fusion.3 = (f32[]{:T(128)}, f32[512,512]{0,1:T(8,128)}) fusion(f32[512,512]{0,1:T(8,128)S(1)} %fusion.63, f32[512,512]{1,0:T(8,128)S(1)} %copy-done.3), kind=kOutput, calls=%fused_computation.8.clone.1 | convolution fusion | flops 1611923456 | bytes 3145732 | tf_op jit(solution)/shard_map/while/body/dot_general | solution.py:41
  174.3 4.7 %convolution_add_fusion.3 = f32[512,512]{0,1:T(8,128)} fusion(f32[512,512]{0,1:T(8,128)} %copy-done.1, f32[512,512]{0,1:T(8,128)} %get-tuple-element.114), kind=kOutput, calls=%fused_computation.1.clone.1 | convolution fusion | flops 1610874880 | bytes 3145728 | tf_op jit(solution)/shard_map/while/body/dot_general | solution.py:43
  179.1 3.5 %convert_subtract_fusion.3 = f32[512,512]{0,1:T(8,128)S(1)} fusion(f32[512,512]{1,0:T(8,128)} %get-tuple-element.129, f32[512,512]{0,1:T(8,128)} %get-tuple-element.122), kind=kOutput, calls=%fused_computation.3.clone.1 | convolution fusion | flops 1611399168 | bytes 3145728 | tf_op jit(solution)/shard_map/while/body/dot_general | solution.py:41
  182.6 3.4 %fusion.63 = f32[512,512]{0,1:T(8,128)S(1)} fusion(f32[512,512]{0,1:T(8,128)} %get-tuple-element.122, f32[512,512]{0,1:T(8,128)S(1)} %convert_subtract_fusion.3), kind=kOutput, calls=%fused_computation.6.clone.1 | convolution fusion | flops 1610874880 | bytes 3145728 | tf_op jit(solution)/shard_map/while/body/dot_general | solution.py:43
  186.0 1.0 copy-done.1
  187.0 3.5 %multiply_reduce_fusion.3 = (f32[]{:T(128)}, f32[512,512]{0,1:T(8,128)}) fusion(f32[512,512]{0,1:T(8,128)S(1)} %fusion.63, f32[512,512]{1,0:T(8,128)S(1)} %copy-done.3), kind=kOutput, calls=%fused_computation.8.clone.1 | convolution fusion | flops 1611923456 | bytes 3145732 | tf_op jit(solution)/shard_map/while/body/dot_general | solution.py:41
  191.1 4.7 %convolution_add_fusion.3 = f32[512,512]{0,1:T(8,128)} fusion(f32[512,512]{0,1:T(8,128)} %copy-done.1, f32[512,512]{0,1:T(8,128)} %get-tuple-element.114), kind=kOutput, calls=%fused_computation.1.clone.1 | convolution fusion | flops 1610874880 | bytes 3145728 | tf_op jit(solution)/shard_map/while/body/dot_general | solution.py:43
  195.9 3.5 %convert_subtract_fusion.3 = f32[512,512]{0,1:T(8,128)S(1)} fusion(f32[512,512]{1,0:T(8,128)} %get-tuple-element.129, f32[512,512]{0,1:T(8,128)} %get-tuple-element.122), kind=kOutput, calls=%fused_computation.3.clone.1 | convolution fusion | flops 1611399168 | bytes 3145728 | tf_op jit(solution)/shard_map/while/body/dot_general | solution.py:41
  199.3 3.4 %fusion.63 = f32[512,512]{0,1:T(8,128)S(1)} fusion(f32[512,512]{0,1:T(8,128)} %get-tuple-element.122, f32[512,512]{0,1:T(8,128)S(1)} %convert_subtract_fusion.3), kind=kOutput, calls=%fused_computation.6.clone.1 | convolution fusion | flops 1610874880 | bytes 3145728 | tf_op jit(solution)/shard_map/while/body/dot_general | solution.py:43
  202.8 0.0 copy-start.1
  202.8 1.0 copy-done.1
  203.8 3.5 %multiply_reduce_fusion.3 = (f32[]{:T(128)}, f32[512,512]{0,1:T(8,128)}) fusion(f32[512,512]{0,1:T(8,128)S(1)} %fusion.63, f32[512,512]{1,0:T(8,128)S(1)} %copy-done.3), kind=kOutput, calls=%fused_computation.8.clone.1 | convolution fusion | flops 1611923456 | bytes 3145732 | tf_op jit(solution)/shard_map/while/body/dot_general | solution.py:41
  207.9 4.7 %convolution_add_fusion.3 = f32[512,512]{0,1:T(8,128)} fusion(f32[512,512]{0,1:T(8,128)} %copy-done.1, f32[512,512]{0,1:T(8,128)} %get-tuple-element.114), kind=kOutput, calls=%fused_computation.1.clone.1 | convolution fusion | flops 1610874880 | bytes 3145728 | tf_op jit(solution)/shard_map/while/body/dot_general | solution.py:43
  212.6 3.5 %convert_subtract_fusion.3 = f32[512,512]{0,1:T(8,128)S(1)} fusion(f32[512,512]{1,0:T(8,128)} %get-tuple-element.129, f32[512,512]{0,1:T(8,128)} %get-tuple-element.122), kind=kOutput, calls=%fused_computation.3.clone.1 | convolution fusion | flops 1611399168 | bytes 3145728 | tf_op jit(solution)/shard_map/while/body/dot_general | solution.py:41
  216.1 3.4 %fusion.63 = f32[512,512]{0,1:T(8,128)S(1)} fusion(f32[512,512]{0,1:T(8,128)} %get-tuple-element.122, f32[512,512]{0,1:T(8,128)S(1)} %convert_subtract_fusion.3), kind=kOutput, calls=%fused_computation.6.clone.1 | convolution fusion | flops 1610874880 | bytes 3145728 | tf_op jit(solution)/shard_map/while/body/dot_general | solution.py:43
  219.6 1.0 copy-done.1
  220.6 3.5 %multiply_reduce_fusion.3 = (f32[]{:T(128)}, f32[512,512]{0,1:T(8,128)}) fusion(f32[512,512]{0,1:T(8,128)S(1)} %fusion.63, f32[512,512]{1,0:T(8,128)S(1)} %copy-done.3), kind=kOutput, calls=%fused_computation.8.clone.1 | convolution fusion | flops 1611923456 | bytes 3145732 | tf_op jit(solution)/shard_map/while/body/dot_general | solution.py:41
  224.7 4.7 %convolution_add_fusion.3 = f32[512,512]{0,1:T(8,128)} fusion(f32[512,512]{0,1:T(8,128)} %copy-done.1, f32[512,512]{0,1:T(8,128)} %get-tuple-element.114), kind=kOutput, calls=%fused_computation.1.clone.1 | convolution fusion | flops 1610874880 | bytes 3145728 | tf_op jit(solution)/shard_map/while/body/dot_general | solution.py:43
  229.4 3.5 %convert_subtract_fusion.3 = f32[512,512]{0,1:T(8,128)S(1)} fusion(f32[512,512]{1,0:T(8,128)} %get-tuple-element.129, f32[512,512]{0,1:T(8,128)} %get-tuple-element.122), kind=kOutput, calls=%fused_computation.3.clone.1 | convolution fusion | flops 1611399168 | bytes 3145728 | tf_op jit(solution)/shard_map/while/body/dot_general | solution.py:41
  232.9 3.4 %fusion.63 = f32[512,512]{0,1:T(8,128)S(1)} fusion(f32[512,512]{0,1:T(8,128)} %get-tuple-element.122, f32[512,512]{0,1:T(8,128)S(1)} %convert_subtract_fusion.3), kind=kOutput, calls=%fused_computation.6.clone.1 | convolution fusion | flops 1610874880 | bytes 3145728 | tf_op jit(solution)/shard_map/while/body/dot_general | solution.py:43
  236.4 1.0 copy-done.1
  237.4 3.5 %multiply_reduce_fusion.3 = (f32[]{:T(128)}, f32[512,512]{0,1:T(8,128)}) fusion(f32[512,512]{0,1:T(8,128)S(1)} %fusion.63, f32[512,512]{1,0:T(8,128)S(1)} %copy-done.3), kind=kOutput, calls=%fused_computation.8.clone.1 | convolution fusion | flops 1611923456 | bytes 3145732 | tf_op jit(solution)/shard_map/while/body/dot_general | solution.py:41
  241.5 4.7 %convolution_add_fusion.3 = f32[512,512]{0,1:T(8,128)} fusion(f32[512,512]{0,1:T(8,128)} %copy-done.1, f32[512,512]{0,1:T(8,128)} %get-tuple-element.114), kind=kOutput, calls=%fused_computation.1.clone.1 | convolution fusion | flops 1610874880 | bytes 3145728 | tf_op jit(solution)/shard_map/while/body/dot_general | solution.py:43
  246.2 3.1 %fusion.23 = f32[512,256]{1,0:T(8,128)S(1)} fusion(f32[512,512]{0,1:T(8,128)} %get-tuple-element.38, f32[512,256]{1,0:T(8,128)S(1)} %fusion.3), kind=kOutput, calls=%fused_computation.43 | convolution fusion | flops 805306368 | bytes 2097152 | tf_op jit(solution)/shard_map/dot_general | solution.py:54
  249.4 2.2 convolution_subtract_fusion
  251.6 1.8 fusion.8
  253.4 0.6 pad_maximum_fusion.4
  (24 shorter events, 0.1 us)
Async XLA Ops:
  6.5 3.2 %copy-start = (bf16[1,96,14336]{2,1,0:T(8,128)(2,1)S(1)}, bf16[1,96,14336]{2,1,0:T(8,128)(2,1)}, u32[]{:S(2)}) copy-start(bf16[1,96,14336]{2,1,0:T(8,128)(2,1)} %param.14) | copy-start | bytes 8257540
  6.5 117.8 %all-gather.3.cloned.1.call-start = ((), (), s32[]{:S(2)}) async-start(), calls=%async_computation | async-start | bytes 13369344 | tf_op jit(solution)/shard_map/all_gather | solution.py:76
  12.5 5.2 %copy-start.7 = (bf16[4096,64]{0,1:T(8,128)(2,1)S(1)}, bf16[4096,64]{0,1:T(8,128)(2,1)}, u32[]{:S(2)}) copy-start(bf16[4096,64]{0,1:T(8,128)(2,1)} %param.16) | copy-start | bytes 1572868
  128.3 15.9 %copy-start.5 = (f32[256,4096]{1,0:T(8,128)}, f32[256,4096]{1,0:T(8,128)S(1)}, u32[]{:S(2)}) copy-start(f32[256,4096]{1,0:T(8,128)S(1)} %get-tuple-element.82) | copy-start | bytes 12582916
  128.4 15.9 %copy-start.6 = (f32[256,4096]{1,0:T(8,128)}, f32[256,4096]{1,0:T(8,128)S(1)}, u32[]{:S(2)}) copy-start(f32[256,4096]{1,0:T(8,128)S(1)} %get-tuple-element.83) | copy-start | bytes 12582916
  146.3 10.7 %copy-start.2 = (f32[512,512]{1,0:T(8,128)}, f32[512,512]{1,0:T(8,128)S(1)}, u32[]{:S(2)}) copy-start(f32[512,512]{1,0:T(8,128)S(1)} %select_add_fusion) | copy-start | bytes 3145732
  162.3 7.9 %copy-start.3 = (f32[512,512]{1,0:T(8,128)S(1)}, f32[512,512]{1,0:T(8,128)}, u32[]{:S(2)}) copy-start(f32[512,512]{1,0:T(8,128)} %get-tuple-element.129) | copy-start | bytes 3145732 | tf_op jit(solution)/shard_map/while
  169.2 1.0 copy-start.1
  179.1 7.9 %copy-start.3 = (f32[512,512]{1,0:T(8,128)S(1)}, f32[512,512]{1,0:T(8,128)}, u32[]{:S(2)}) copy-start(f32[512,512]{1,0:T(8,128)} %get-tuple-element.129) | copy-start | bytes 3145732 | tf_op jit(solution)/shard_map/while
  186.0 1.0 copy-start.1
  195.8 7.9 %copy-start.3 = (f32[512,512]{1,0:T(8,128)S(1)}, f32[512,512]{1,0:T(8,128)}, u32[]{:S(2)}) copy-start(f32[512,512]{1,0:T(8,128)} %get-tuple-element.129) | copy-start | bytes 3145732 | tf_op jit(solution)/shard_map/while
  202.8 1.0 copy-start.1
  212.6 7.9 %copy-start.3 = (f32[512,512]{1,0:T(8,128)S(1)}, f32[512,512]{1,0:T(8,128)}, u32[]{:S(2)}) copy-start(f32[512,512]{1,0:T(8,128)} %get-tuple-element.129) | copy-start | bytes 3145732 | tf_op jit(solution)/shard_map/while
  219.6 1.0 copy-start.1
  229.4 7.9 %copy-start.3 = (f32[512,512]{1,0:T(8,128)S(1)}, f32[512,512]{1,0:T(8,128)}, u32[]{:S(2)}) copy-start(f32[512,512]{1,0:T(8,128)} %get-tuple-element.129) | copy-start | bytes 3145732 | tf_op jit(solution)/shard_map/while
  236.4 1.0 copy-start.1
  246.2 5.3 %copy-start.4 = (f32[512,512]{0,1:T(8,128)S(1)}, f32[512,512]{0,1:T(8,128)}, u32[]{:S(2)}) copy-start(f32[512,512]{0,1:T(8,128)} %get-tuple-element.38) | copy-start | bytes 3145732
Sparse Core Ops, SparseCore 0:
  42.2 82.0 all-gather.2
where the time goes:
time: 262 us; the launch traced here: 261 us
  matrix products  121 us (46%)
  waiting for transfers between devices  82.2 us (31%)
  blocking collectives  20.5 us (8%)
  between operations  14.3 us (5%)
  local copies, waits for them, and re-layouts  13.3 us (5%)
  other arithmetic  6.29 us (2%)
  loops' own time  3.45 us (1%)
    all_gather x1, waiting for transfers between devices, body(): everyone = lax.all_gather(within, AXES[0], axis=0, tiled=True)  82.2 us
    dot_general x10, matrix products, one_step(): return (inverse + jnp.dot(inverse, remainder, precision=HIGHEST), residual)  40.8 us
    dot_general x10, matrix products, one_step(): remainder = eye - jnp.dot(system, inverse, precision=HIGHEST)  34.9 us
    all_gather x1, blocking collectives, body(): within = lax.all_gather(both.reshape(1, -1), AXES[1], axis=0, tiled=True)  20.5 us
    dot_general x1, matrix products, body(): gram_matrix = jnp.dot(all_train, all_train.T, precision=HIGHEST)  15.9 us
    dot_general x1, matrix products, body(): products = jnp.dot(all_train, pieces[block_rows].T, precision=HIGHEST)  10.6 us
    dot_general x2, matrix products, sketch_terms(): jnp.dot(outgrad.reshape(proof_count * token_count, -1), proj_out, preferr...  7.41 us
  transfers between devices with their start and end apart: 1, of which 1 were waited for; matrix products, arithmetic and copies ran while one was open for 0% of the time, Pallas kernels for 0%

commit v1 on v0

--- a/solution.py
+++ b/solution.py
@@ -44,9 +44,10 @@
 
     def advance(carry):
         step, inverse, _ = carry
-        inverse, _ = one_step(inverse)
+        for _ in range(3):
+            inverse, _ = one_step(inverse)
         inverse, residual = one_step(inverse)
-        return step + 2, inverse, residual
+        return step + 4, inverse, residual
 
     _, inverse, _ = lax.while_loop(
         going, advance, (jnp.int32(0), start, jnp.array(jnp.inf, system.dtype))

time: 262 us -> 247 us (0.943)
  matrix products: 121 us -> 113 us
  local copies, waits for them, and re-layouts: 13.3 us -> 8.45 us
    dot_general x10 -> x12, matrix products: 40.8 us -> 35.7 us  [one_step(): return (inverse + jnp.dot(inverse, remainder, precision=HIGHEST), residual)]
    while x20 -> x12, local copies, waits for them, and re-layouts: 4.87 us -> 0.02 us
    dot_general x10 -> x12, matrix products: 34.9 us -> 32.1 us  [one_step(): remainder = eye - jnp.dot(system, inverse, precision=HIGHEST)]
where the time goes in v1:
time: 247 us
  matrix products  113 us (46%)
  waiting for transfers between devices  82.2 us (33%)
  blocking collectives  20.5 us (8%)
  between operations  14.3 us (6%)
  local copies, waits for them, and re-layouts  8.45 us (3%)
  other arithmetic  6.29 us (3%)
    all_gather x1, waiting for transfers between devices, body(): everyone = lax.all_gather(within, AXES[0], axis=0, tiled=True)  82.2 us
    dot_general x12, matrix products, one_step(): return (inverse + jnp.dot(inverse, remainder, precision=HIGHEST), residual)  35.7 us
    dot_general x12, matrix products, one_step(): remainder = eye - jnp.dot(system, inverse, precision=HIGHEST)  32.1 us
    all_gather x1, blocking collectives, body(): within = lax.all_gather(both.reshape(1, -1), AXES[1], axis=0, tiled=True)  20.5 us
    dot_general x1, matrix products, body(): gram_matrix = jnp.dot(all_train, all_train.T, precision=HIGHEST)  15.9 us
    dot_general x1, matrix products, body(): products = jnp.dot(all_train, pieces[block_rows].T, precision=HIGHEST)  10.6 us
    dot_general x2, matrix products, sketch_terms(): jnp.dot(outgrad.reshape(proof_count * token_count, -1), proj_out, preferr...  7.41 us
  transfers between devices with their start and end apart: 1, of which 1 were waited for; matrix products, arithmetic and copies ran while one was open for 0% of the time, Pallas kernels for 0%

profile of v1, /device:TPU:1, one launch (start us, length us, event | category | flops | bytes accessed | tf_op | source)
XLA Modules:
  0.0 246.9 jit_solution(12028360750653401418)
XLA Ops:
  6.5 0.0 copy-start
  6.5 0.0 all-gather.3.cloned.1.call-start
  6.5 0.8 convert_bitcast_fusion
  7.3 0.7 convert_element_type.32
  8.1 0.1 convert_element_type.33
  8.1 1.6 fusion.13
  9.8 0.0 copy-done
  9.8 2.4 fusion.9
  12.2 0.2 fusion.22
  12.4 0.1 reshape.66
  12.5 0.0 copy-start.7
  12.5 5.1 %convolution_multiply_fusion = f32[192,64]{0,1:T(8,128)S(1)} fusion(bf16[192,14336]{1,0:T(8,128)(2,1)} %bitcast.103, bf16[14336,64]{0,1:T(8,128)(2,1)} %param.17, f32[192]{0:T(256)S(1)} %convert_element_type.33), kind=kOutput, calls=%fused_computation.24 | convolution fusion | flops 352333824 | bytes 7389952 | tf_op jit(solution)/shard_map/dot_general | solution.py:18
  17.6 0.1 reshape.62
  17.7 2.1 fusion.15
  19.8 0.2 fusion.17
  20.0 0.1 reshape.63
  20.2 0.1 reshape.68
  20.2 20.5 %all-gather = f32[16,1,12288]{2,1,0:T(1,128)S(1)} all-gather(f32[1,1,12288]{2,1,0:T(1,128)S(1)} %reshape.68), channel_id=1, replica_groups=mesh['train'=16,'query'=16] {'query'}, dimensions={0}, use_global_device_ids=true | all-gather | bytes 835584 | tf_op jit(solution)/shard_map/all_gather | solution.py:76
  40.7 1.4 copy.26
  42.1 0.0 all-gather.3.cloned.1.call-update
  42.1 82.2 %all-gather.3.cloned.1.call-done = f32[256,12288]{1,0:T(8,128)} async-done(((f32[16,12288]{1,0:T(8,128)}), f32[256,12288]{1,0:T(8,128)}) %all-gather.3.cloned.1.call-update) | async-done | bytes 12582928 | tf_op jit(solution)/shard_map/all_gather | solution.py:77
  124.3 4.0 %fusion.21 = (f32[256,4096]{1,0:T(8,128)S(1)}, f32[256,4096]{1,0:T(8,128)S(1)}) fusion(f32[256,12288]{1,0:T(8,128)} %all-gather.3.cloned.1.call-done), kind=kLoop, calls=%fused_computation.47 | loop fusion | bytes 16777216 | tf_op jit(solution)/shard_map/slice | solution.py:79
  128.4 15.9 %select_reduce_fusion.1 = (f32[]{:T(128)}, f32[512,512]{1,0:T(8,128)}) fusion(f32[256,4096]{1,0:T(8,128)S(1)} %get-tuple-element.91, f32[256,4096]{1,0:T(8,128)S(1)} %get-tuple-element.90), kind=kOutput, calls=%fused_computation.29 | convolution fusion | flops 12887785472 | bytes 9437188 | tf_op jit(solution)/shard_map/dot_general | solution.py:81
  144.3 0.0 copy-done.5
  144.9 1.3 select_add_fusion
  146.3 0.0 copy-start.1
  146.3 10.6 %fusion.3 = f32[512,256]{1,0:T(8,128)S(1)} fusion(f32[256,4096]{1,0:T(8,128)} %copy-done.6, f32[256,4096]{1,0:T(8,128)} %copy-done.5, f32[256,12288]{1,0:T(8,128)} %all-gather.3.cloned.1.call-done), kind=kOutput, calls=%fused_computation.16 | convolution fusion | flops 6444548096 | bytes 13107200 | tf_op jit(solution)/shard_map/dot_general | solution.py:82
  156.9 0.1 select_reduce_fusion
  157.0 0.3 multiply_reduce_fusion.1
  157.3 0.6 reduce_max.9
  158.0 0.6 multiply_divide_fusion
  158.6 1.1 fusion.12
  159.7 2.5 %copy.18 = f32[512,512]{0,1:T(8,128)} copy(f32[512,512]{1,0:T(8,128)} %fusion.12) | data formatting | bytes 2097152
  162.3 70.0 %while.14 = (s32[]{:T(128)}, f32[512,512]{0,1:T(8,128)}, f32[]{:T(128)}, f32[512,512]{1,0:T(8,128)}, s32[]{:T(128)}) while((s32[]{:T(128)}, f32[512,512]{0,1:T(8,128)}, f32[]{:T(128)}, f32[512,512]{1,0:T(8,128)}, s32[]{:T(128)}) %tuple.39), condition=%wide.region_6.0_spmd.clone.clone, body=%wide.region_4.0_spmd.clone.clone.sunk | while | flops 12889620480 | bytes 33554572 | solution.py:52
  162.3 3.5 %convert_subtract_fusion.7 = f32[512,512]{0,1:T(8,128)S(1)} fusion(f32[512,512]{1,0:T(8,128)} %get-tuple-element.137, f32[512,512]{0,1:T(8,128)} %get-tuple-element.130), kind=kOutput, calls=%fused_computation.4.clone.1 | convolution fusion | flops 1611399168 | bytes 3145728 | tf_op jit(solution)/shard_map/while/body/dot_general | solution.py:41
  165.8 3.4 %fusion.87 = f32[512,512]{0,1:T(8,128)S(1)} fusion(f32[512,512]{0,1:T(8,128)} %get-tuple-element.130, f32[512,512]{0,1:T(8,128)S(1)} %convert_subtract_fusion.7), kind=kOutput, calls=%fused_computation.12.clone.1 | convolution fusion | flops 1610874880 | bytes 3145728 | tf_op jit(solution)/shard_map/while/body/dot_general | solution.py:43
  169.2 1.9 convert_subtract_fusion.8
  171.1 1.9 convolution_add_fusion.7
  173.0 1.9 convert_subtract_fusion.9
  174.8 1.9 convolution_add_fusion.8
  176.7 3.5 %multiply_reduce_fusion.3 = (f32[]{:T(128)}, f32[512,512]{0,1:T(8,128)}) fusion(f32[512,512]{0,1:T(8,128)S(1)} %convolution_add_fusion.8, f32[512,512]{1,0:T(8,128)S(1)} %copy-done.2), kind=kOutput, calls=%fused_computation.14.clone.1 | convolution fusion | flops 1611923456 | bytes 3145732 | tf_op jit(solution)/shard_map/while/body/dot_general | solution.py:41
  180.9 4.7 %convolution_add_fusion.9 = f32[512,512]{0,1:T(8,128)} fusion(f32[512,512]{0,1:T(8,128)} %copy-done.3, f32[512,512]{0,1:T(8,128)} %get-tuple-element.122), kind=kOutput, calls=%fused_computation.5.clone.1 | convolution fusion | flops 1610874880 | bytes 3145728 | tf_op jit(solution)/shard_map/while/body/dot_general | solution.py:43
  185.6 3.5 %convert_subtract_fusion.7 = f32[512,512]{0,1:T(8,128)S(1)} fusion(f32[512,512]{1,0:T(8,128)} %get-tuple-element.137, f32[512,512]{0,1:T(8,128)} %get-tuple-element.130), kind=kOutput, calls=%fused_computation.4.clone.1 | convolution fusion | flops 1611399168 | bytes 3145728 | tf_op jit(solution)/shard_map/while/body/dot_general | solution.py:41
  189.1 3.4 %fusion.87 = f32[512,512]{0,1:T(8,128)S(1)} fusion(f32[512,512]{0,1:T(8,128)} %get-tuple-element.130, f32[512,512]{0,1:T(8,128)S(1)} %convert_subtract_fusion.7), kind=kOutput, calls=%fused_computation.12.clone.1 | convolution fusion | flops 1610874880 | bytes 3145728 | tf_op jit(solution)/shard_map/while/body/dot_general | solution.py:43
  192.5 0.0 copy-done.2
  192.5 1.9 convert_subtract_fusion.8
  194.4 1.9 convolution_add_fusion.7
  196.3 1.9 convert_subtract_fusion.9
  198.2 1.9 convolution_add_fusion.8
  200.1 3.5 %multiply_reduce_fusion.3 = (f32[]{:T(128)}, f32[512,512]{0,1:T(8,128)}) fusion(f32[512,512]{0,1:T(8,128)S(1)} %convolution_add_fusion.8, f32[512,512]{1,0:T(8,128)S(1)} %copy-done.2), kind=kOutput, calls=%fused_computation.14.clone.1 | convolution fusion | flops 1611923456 | bytes 3145732 | tf_op jit(solution)/shard_map/while/body/dot_general | solution.py:41
  204.2 4.7 %convolution_add_fusion.9 = f32[512,512]{0,1:T(8,128)} fusion(f32[512,512]{0,1:T(8,128)} %copy-done.3, f32[512,512]{0,1:T(8,128)} %get-tuple-element.122), kind=kOutput, calls=%fused_computation.5.clone.1 | convolution fusion | flops 1610874880 | bytes 3145728 | tf_op jit(solution)/shard_map/while/body/dot_general | solution.py:43
  208.9 3.5 %convert_subtract_fusion.7 = f32[512,512]{0,1:T(8,128)S(1)} fusion(f32[512,512]{1,0:T(8,128)} %get-tuple-element.137, f32[512,512]{0,1:T(8,128)} %get-tuple-element.130), kind=kOutput, calls=%fused_computation.4.clone.1 | convolution fusion | flops 1611399168 | bytes 3145728 | tf_op jit(solution)/shard_map/while/body/dot_general | solution.py:41
  212.4 3.4 %fusion.87 = f32[512,512]{0,1:T(8,128)S(1)} fusion(f32[512,512]{0,1:T(8,128)} %get-tuple-element.130, f32[512,512]{0,1:T(8,128)S(1)} %convert_subtract_fusion.7), kind=kOutput, calls=%fused_computation.12.clone.1 | convolution fusion | flops 1610874880 | bytes 3145728 | tf_op jit(solution)/shard_map/while/body/dot_general | solution.py:43
  215.9 1.9 convert_subtract_fusion.8
  217.7 1.9 convolution_add_fusion.7
  219.6 1.9 convert_subtract_fusion.9
  221.5 1.9 convolution_add_fusion.8
  223.4 3.5 %multiply_reduce_fusion.3 = (f32[]{:T(128)}, f32[512,512]{0,1:T(8,128)}) fusion(f32[512,512]{0,1:T(8,128)S(1)} %convolution_add_fusion.8, f32[512,512]{1,0:T(8,128)S(1)} %copy-done.2), kind=kOutput, calls=%fused_computation.14.clone.1 | convolution fusion | flops 1611923456 | bytes 3145732 | tf_op jit(solution)/shard_map/while/body/dot_general | solution.py:41
  226.9 0.0 copy-done.3
  227.5 4.7 %convolution_add_fusion.9 = f32[512,512]{0,1:T(8,128)} fusion(f32[512,512]{0,1:T(8,128)} %copy-done.3, f32[512,512]{0,1:T(8,128)} %get-tuple-element.122), kind=kOutput, calls=%fused_computation.5.clone.1 | convolution fusion | flops 1610874880 | bytes 3145728 | tf_op jit(solution)/shard_map/while/body/dot_general | solution.py:43
  232.3 3.1 %fusion.23 = f32[512,256]{1,0:T(8,128)S(1)} fusion(f32[512,512]{0,1:T(8,128)} %get-tuple-element.44, f32[512,256]{1,0:T(8,128)S(1)} %fusion.3), kind=kOutput, calls=%fused_computation.49 | convolution fusion | flops 805306368 | bytes 2097152 | tf_op jit(solution)/shard_map/dot_general | solution.py:55
  235.4 2.2 convolution_subtract_fusion
  237.6 1.8 fusion.8
  239.5 0.6 pad_maximum_fusion.4
  (20 shorter events, 0.1 us)
Async XLA Ops:
  6.5 3.2 %copy-start = (bf16[1,96,14336]{2,1,0:T(8,128)(2,1)S(1)}, bf16[1,96,14336]{2,1,0:T(8,128)(2,1)}, u32[]{:S(2)}) copy-start(bf16[1,96,14336]{2,1,0:T(8,128)(2,1)} %param.14) | copy-start | bytes 8257540
  6.5 117.8 %all-gather.3.cloned.1.call-start = ((), (), s32[]{:S(2)}) async-start(), calls=%async_computation | async-start | bytes 13369344 | tf_op jit(solution)/shard_map/all_gather | solution.py:77
  12.5 5.2 %copy-start.7 = (bf16[4096,64]{0,1:T(8,128)(2,1)S(1)}, bf16[4096,64]{0,1:T(8,128)(2,1)}, u32[]{:S(2)}) copy-start(bf16[4096,64]{0,1:T(8,128)(2,1)} %param.16) | copy-start | bytes 1572868
  128.3 15.9 %copy-start.5 = (f32[256,4096]{1,0:T(8,128)}, f32[256,4096]{1,0:T(8,128)S(1)}, u32[]{:S(2)}) copy-start(f32[256,4096]{1,0:T(8,128)S(1)} %get-tuple-element.90) | copy-start | bytes 12582916
  128.4 15.9 %copy-start.6 = (f32[256,4096]{1,0:T(8,128)}, f32[256,4096]{1,0:T(8,128)S(1)}, u32[]{:S(2)}) copy-start(f32[256,4096]{1,0:T(8,128)S(1)} %get-tuple-element.91) | copy-start | bytes 12582916
  146.3 10.7 %copy-start.1 = (f32[512,512]{1,0:T(8,128)}, f32[512,512]{1,0:T(8,128)S(1)}, u32[]{:S(2)}) copy-start(f32[512,512]{1,0:T(8,128)S(1)} %select_add_fusion) | copy-start | bytes 3145732
  162.3 6.9 %copy-start.2 = (f32[512,512]{1,0:T(8,128)S(1)}, f32[512,512]{1,0:T(8,128)}, u32[]{:S(2)}) copy-start(f32[512,512]{1,0:T(8,128)} %get-tuple-element.137) | copy-start | bytes 3145732 | tf_op jit(solution)/shard_map/while
  176.7 3.5 %copy-start.3 = (f32[512,512]{0,1:T(8,128)}, f32[512,512]{0,1:T(8,128)S(1)}, u32[]{:S(2)}) copy-start(f32[512,512]{0,1:T(8,128)S(1)} %convolution_add_fusion.8) | copy-start | bytes 3145732 | tf_op jit(solution)/shard_map/while
  185.6 6.9 %copy-start.2 = (f32[512,512]{1,0:T(8,128)S(1)}, f32[512,512]{1,0:T(8,128)}, u32[]{:S(2)}) copy-start(f32[512,512]{1,0:T(8,128)} %get-tuple-element.137) | copy-start | bytes 3145732 | tf_op jit(solution)/shard_map/while
  200.0 3.5 %copy-start.3 = (f32[512,512]{0,1:T(8,128)}, f32[512,512]{0,1:T(8,128)S(1)}, u32[]{:S(2)}) copy-start(f32[512,512]{0,1:T(8,128)S(1)} %convolution_add_fusion.8) | copy-start | bytes 3145732 | tf_op jit(solution)/shard_map/while
  208.9 6.9 %copy-start.2 = (f32[512,512]{1,0:T(8,128)S(1)}, f32[512,512]{1,0:T(8,128)}, u32[]{:S(2)}) copy-start(f32[512,512]{1,0:T(8,128)} %get-tuple-element.137) | copy-start | bytes 3145732 | tf_op jit(solution)/shard_map/while
  223.4 3.5 %copy-start.3 = (f32[512,512]{0,1:T(8,128)}, f32[512,512]{0,1:T(8,128)S(1)}, u32[]{:S(2)}) copy-start(f32[512,512]{0,1:T(8,128)S(1)} %convolution_add_fusion.8) | copy-start | bytes 3145732 | tf_op jit(solution)/shard_map/while
  232.3 5.3 %copy-start.4 = (f32[512,512]{0,1:T(8,128)S(1)}, f32[512,512]{0,1:T(8,128)}, u32[]{:S(2)}) copy-start(f32[512,512]{0,1:T(8,128)} %get-tuple-element.44) | copy-start | bytes 3145732
Sparse Core Ops, SparseCore 0:
  42.2 82.0 all-gather.2
